TPU v7x, 32 devices: a whole 2x2x4 slice. The times are simulated.
32 devices in a mesh: sx: 8 (over z, y), sy: 4 (over x, core).
Axes of the slice: x: 2, y: 2, z: 4, core: 2. Of those that a mesh axis runs over, the one named last changes fastest.
Arguments:
- schur: bfloat16 [8, 4096, 4096], P('sx', 'sy'), as said below
- precond: bfloat16 [8, 4096, 4096], P('sx', 'sy'), as said below
- right_side: float32 [8, 32, 2048], P('sx', None, 'sy')
- matching: int32 [8, 2048], P('sx', 'sy'), may hold values from 0 to 511, as said below
Outputs:
- solution: float32 [8, 32, 2048], P('sx', None, 'sy')
- residual: float32 [8, 32, 2048], P('sx', None, 'sy')
Inputs may be any that keep to these rules, and one draw needn't show every extreme that they name: `schur`: each subdomain's matrix is symmetric positive definite. `precond`: each subdomain's matrix is symmetric positive definite. `matching`: each aligned block of 512 entries of a row is a permutation of 0 to 511.
All inputs are finite; a program needn't handle non-finite values.
Results may differ from a plain program's by a relative error of at most 0.007.
The roundings to bfloat16 on the way count: a program that leaves them out, or rounds other values in their place, can miss the bound.
Values may be sent and summed in bfloat16 or wider, within the bound.
No kernel may reach another device: no remote copies, remote signals or barrier semaphores. Data moves between devices by JAX's collectives and lax.ppermute only.
A program may use at most 64 MiB of HBM per device.

v0:
```python
import jax
import jax.numpy as jnp
from jax import lax
from jax.sharding import PartitionSpec as P

ITERS = 2


def passed_along(block, axis, distance):
    devices = range(lax.axis_size(axis))
    route = [((i - distance) % len(devices), i) for i in devices]
    return lax.ppermute(block, axis, route)


def apply_op(matrix, block, match_loc, inverse):
    rows_here = matrix.shape[0]
    half = rows_here // 2
    sent = jnp.take(block, match_loc, axis=1)
    right_part = passed_along(sent, "sx", -1)
    local = jnp.concatenate([block, right_part], axis=1)
    prod = lax.dot_general(
        lax.all_gather(local, "sy", axis=1, tiled=True),
        matrix,
        (((1,), (1,)), ((), ())),
        preferred_element_type=jnp.float32,
    )
    left_out = prod[:, :half]
    right_out = prod[:, half:]
    came = passed_along(right_out, "sx", 1)
    return left_out + jnp.take(came, inverse, axis=1)


def gram(first, second):
    partial_sum = jnp.dot(first, second.T, precision=lax.Precision.HIGHEST)
    total = lax.psum(partial_sum, ("sx", "sy"))
    return 0.5 * (total + total.T)


def solve_spd(matrix, rhs):
    lower = jnp.linalg.cholesky(matrix)
    return jax.scipy.linalg.cho_solve((lower, True), rhs)


def combine(coeff, block):
    return jnp.dot(coeff.T, block, precision=lax.Precision.HIGHEST)


def shards(schur, precond, right_side, matching):
    schur_rows = schur[0]
    precond_rows = precond[0]
    match_loc = matching[0]
    inverse = jnp.argsort(match_loc)
    residual = right_side[0]
    solution = jnp.zeros_like(residual)
    search = apply_op(precond_rows, residual.astype(jnp.bfloat16), match_loc, inverse)
    gamma = gram(residual, search)
    for step in range(ITERS):
        image = apply_op(schur_rows, search.astype(jnp.bfloat16), match_loc, inverse)
        delta = gram(search, image)
        alpha = solve_spd(delta, gamma)
        solution = solution + combine(alpha, search)
        residual = residual - combine(alpha, image)
        if step + 1 < ITERS:
            precd = apply_op(precond_rows, residual.astype(jnp.bfloat16), match_loc, inverse)
            gnew = gram(residual, precd)
            beta = solve_spd(gamma, gnew)
            search = precd + combine(beta, search)
            gamma = gnew
    return (solution[None], residual[None])


def solution(mesh):
    in_specs = (P("sx", "sy", None), P("sx", "sy", None), P("sx", None, "sy"), P("sx", "sy"))
    out_specs = (P("sx", None, "sy"), P("sx", None, "sy"))
    return jax.shard_map(shards, mesh=mesh, in_specs=in_specs, out_specs=out_specs, check_vma=False)
```

profile of v0, /device:TPU:0, one launch (start us, length us, event | category | flops | bytes accessed | tf_op | source)
XLA Modules:
  0.0 250.3 jit_solution(12864554921434175186)
XLA Ops:
  4.4 6.1 %collective-permute-start = (bf16[32,512]{1,0:T(8,128)(2,1)S(1)}, bf16[32,512]{1,0:T(8,128)(2,1)S(1)}, u32[]{:S(2)}, u32[]{:S(2)}) collective-permute-start(bf16[32,512]{1,0:T(8,128)(2,1)S(1)} %select_bitcast_fusion.3), channel_id=1, source_target_pairs={{4,0},{8,4},{12,8},{16,12},{20,16},{24,20},{28,24},{0,28},{5,1},{9... | collective-permute-start | bytes 98312 | tf_op jit(solution)/shard_map/ppermute | solution.py:12
  10.5 4.4 %sort.17 = (s32[512]{0:T(512)}, s32[512]{0:T(512)S(1)}) sort(s32[512]{0:T(512)} %bitcast.121, s32[512]{0:T(512)S(1)} %iota.35), dimensions={0}, to_apply=%region_0.2 | sort | flops 4608 | bytes 8192 | tf_op jit(solution)/shard_map/jit(argsort)/sort | solution.py:52
  15.0 5.8 %all_gather.12 = bf16[32,4096]{1,0:T(8,128)(2,1)S(1)} all-gather(bf16[32,1024]{1,0:T(8,128)(2,1)S(1)} %pad_maximum_fusion), channel_id=1, replica_groups=mesh['sx'=8,'sy'=4] {'sy'}, dimensions={1}, use_global_device_ids=true | all-gather | bytes 327680 | tf_op jit(solution)/shard_map/all_gather | solution.py:22
  20.8 6.0 %fusion.6 = f32[32,1024]{1,0:T(8,128)S(1)} fusion(bf16[32,4096]{1,0:T(8,128)(2,1)S(1)} %all_gather.12, bf16[1,1024,4096]{2,1,0:T(8,128)(2,1)} %param.12), kind=kOutput, calls=%fused_computation.14 | convolution fusion | flops 268435456 | bytes 8781824 | tf_op jit(solution)/shard_map/dot_general | solution.py:21
  26.9 7.0 %collective-permute-done.1 = f32[32,512]{1,0:T(8,128)S(1)} collective-permute-done((f32[32,512]{1,0:T(8,128)S(1)}, f32[32,512]{1,0:T(8,128)S(1)}, u32[]{:S(2)}, u32[]{:S(2)}) %collective-permute-start.1) | collective-permute-done | bytes 65568 | tf_op jit(solution)/shard_map/ppermute | solution.py:12
  36.8 3.9 %collective-permute-done.2 = bf16[32,512]{1,0:T(8,128)(2,1)S(1)} collective-permute-done((bf16[32,512]{1,0:T(8,128)(2,1)S(1)}, bf16[32,512]{1,0:T(8,128)(2,1)S(1)}, u32[]{:S(2)}, u32[]{:S(2)}) %collective-permute-start.2) | collective-permute-done | bytes 32800 | tf_op jit(solution)/shard_map/ppermute | solution.py:12
  40.7 5.8 %all_gather.13 = bf16[32,4096]{1,0:T(8,128)(2,1)S(1)} all-gather(bf16[32,1024]{1,0:T(8,128)(2,1)S(1)} %pad_maximum_fusion.1), channel_id=1, replica_groups=mesh['sx'=8,'sy'=4] {'sy'}, dimensions={1}, use_global_device_ids=true | all-gather | bytes 327680 | tf_op jit(solution)/shard_map/all_gather | solution.py:22
  46.5 6.0 %fusion.2 = f32[32,1024]{1,0:T(8,128)S(1)} fusion(bf16[32,4096]{1,0:T(8,128)(2,1)S(1)} %all_gather.13, bf16[1,1024,4096]{2,1,0:T(8,128)(2,1)} %param.11), kind=kOutput, calls=%fused_computation.10 | convolution fusion | flops 268435456 | bytes 8781824 | tf_op jit(solution)/shard_map/dot_general | solution.py:21
  52.8 6.8 %collective-permute-done.3 = f32[32,512]{1,0:T(8,128)S(1)} collective-permute-done((f32[32,512]{1,0:T(8,128)S(1)}, f32[32,512]{1,0:T(8,128)S(1)}, u32[]{:S(2)}, u32[]{:S(2)}) %collective-permute-start.3) | collective-permute-done | bytes 65568 | tf_op jit(solution)/shard_map/ppermute | solution.py:12
  61.1 37.1 %all-reduce = (f32[32,32]{1,0:T(8,128)S(1)}, f32[32,32]{1,0:T(8,128)S(1)}) all-reduce(f32[32,32]{1,0:T(8,128)S(1)} %convolution_bitcast_fusion, f32[32,32]{1,0:T(8,128)S(1)} %fusion.11), channel_id=1, replica_groups=mesh['sx'=8,'sy'=4] {'sx','sy'}, use_global_device_ids=true, to_apply=%region_4.8 | all-reduce | flops 2048 | bytes 16384 | tf_op jit(solution)/shard_map/psum | solution.py:35
  98.4 2.9 %cholesky.59 = f32[32,32]{1,0:T(8,128)S(1)} custom-call(f32[32,32]{1,0:T(8,128)S(1)} %fusion.34), custom_call_target="Cholesky" | custom-call | tf_op jit(solution)/shard_map/jit(cholesky)/cholesky | solution.py:40
  105.8 2.9 %cholesky.70 = f32[32,32]{1,0:T(8,128)S(1)} custom-call(f32[32,32]{1,0:T(8,128)S(1)} %fusion.28), custom_call_target="Cholesky" | custom-call | tf_op jit(solution)/shard_map/jit(cholesky)/cholesky | solution.py:40
  110.4 4.1 %collective-permute-start.4 = (bf16[32,512]{1,0:T(8,128)(2,1)S(1)}, bf16[32,512]{1,0:T(8,128)(2,1)S(1)}, u32[]{:S(2)}, u32[]{:S(2)}) collective-permute-start(bf16[32,512]{1,0:T(8,128)(2,1)S(1)} %select_bitcast_fusion.1), channel_id=1, source_target_pairs={{4,0},{8,4},{12,8},{16,12},{20,16},{24,20},{28,24},{0,28},{5,1},{9... | collective-permute-start | bytes 98312 | tf_op jit(solution)/shard_map/ppermute | solution.py:12
  116.0 5.8 %all_gather.14 = bf16[32,4096]{1,0:T(8,128)(2,1)S(1)} all-gather(bf16[32,1024]{1,0:T(8,128)(2,1)S(1)} %pad_maximum_fusion.2), channel_id=1, replica_groups=mesh['sx'=8,'sy'=4] {'sy'}, dimensions={1}, use_global_device_ids=true | all-gather | bytes 327680 | tf_op jit(solution)/shard_map/all_gather | solution.py:22
  121.8 6.0 %fusion.4 = f32[32,1024]{1,0:T(8,128)S(1)} fusion(bf16[32,4096]{1,0:T(8,128)(2,1)S(1)} %all_gather.14, bf16[1,1024,4096]{2,1,0:T(8,128)(2,1)} %param.12), kind=kOutput, calls=%fused_computation.12 | convolution fusion | flops 268435456 | bytes 8781824 | tf_op jit(solution)/shard_map/dot_general | solution.py:21
  130.2 2.4 custom-call.10
  132.6 3.0 %collective-permute-done.5 = f32[32,512]{1,0:T(8,128)S(1)} collective-permute-done((f32[32,512]{1,0:T(8,128)S(1)}, f32[32,512]{1,0:T(8,128)S(1)}, u32[]{:S(2)}, u32[]{:S(2)}) %collective-permute-start.5) | collective-permute-done | bytes 65568 | tf_op jit(solution)/shard_map/ppermute | solution.py:12
  137.1 38.3 %psum.30 = f32[32,32]{1,0:T(8,128)S(1)} all-reduce(f32[32,32]{1,0:T(8,128)S(1)} %fusion.12), channel_id=1, replica_groups=mesh['sx'=8,'sy'=4] {'sx','sy'}, use_global_device_ids=true, to_apply=%region_5.10 | all-reduce | flops 1024 | bytes 8192 | tf_op jit(solution)/shard_map/psum | solution.py:35
  177.7 3.4 %collective-permute-start.6 = (bf16[32,512]{1,0:T(8,128)(2,1)S(1)}, bf16[32,512]{1,0:T(8,128)(2,1)S(1)}, u32[]{:S(2)}, u32[]{:S(2)}) collective-permute-start(bf16[32,512]{1,0:T(8,128)(2,1)S(1)} %select_bitcast_fusion), channel_id=1, source_target_pairs={{4,0},{8,4},{12,8},{16,12},{20,16},{24,20},{28,24},{0,28},{5,1},{9... | collective-permute-start | bytes 98312 | tf_op jit(solution)/shard_map/ppermute | solution.py:12
  182.7 5.8 %all_gather.15 = bf16[32,4096]{1,0:T(8,128)(2,1)S(1)} all-gather(bf16[32,1024]{1,0:T(8,128)(2,1)S(1)} %pad_maximum_fusion.3), channel_id=1, replica_groups=mesh['sx'=8,'sy'=4] {'sy'}, dimensions={1}, use_global_device_ids=true | all-gather | bytes 327680 | tf_op jit(solution)/shard_map/all_gather | solution.py:22
  188.4 6.0 %fusion = f32[32,1024]{1,0:T(8,128)S(1)} fusion(bf16[32,4096]{1,0:T(8,128)(2,1)S(1)} %all_gather.15, bf16[1,1024,4096]{2,1,0:T(8,128)(2,1)} %param.11), kind=kOutput, calls=%fused_computation.8 | convolution fusion | flops 268435456 | bytes 8781824 | tf_op jit(solution)/shard_map/dot_general | solution.py:21
  196.9 5.1 %collective-permute-done.7 = f32[32,512]{1,0:T(8,128)S(1)} collective-permute-done((f32[32,512]{1,0:T(8,128)S(1)}, f32[32,512]{1,0:T(8,128)S(1)}, u32[]{:S(2)}, u32[]{:S(2)}) %collective-permute-start.7) | collective-permute-done | bytes 65568 | tf_op jit(solution)/shard_map/ppermute | solution.py:12
  203.6 37.7 %psum.31 = f32[32,32]{1,0:T(8,128)S(1)} all-reduce(f32[32,32]{1,0:T(8,128)S(1)} %fusion.13), channel_id=1, replica_groups=mesh['sx'=8,'sy'=4] {'sx','sy'}, use_global_device_ids=true, to_apply=%region_6.11 | all-reduce | flops 1024 | bytes 8192 | tf_op jit(solution)/shard_map/psum | solution.py:35
  241.4 2.9 %cholesky.81 = f32[32,32]{1,0:T(8,128)S(1)} custom-call(f32[32,32]{1,0:T(8,128)S(1)} %fusion.21), custom_call_target="Cholesky" | custom-call | tf_op jit(solution)/shard_map/jit(cholesky)/cholesky | solution.py:40
  (93 shorter events, 34.2 us)
Async XLA Ops:
  4.4 10.5 %collective-permute-start = (bf16[32,512]{1,0:T(8,128)(2,1)S(1)}, bf16[32,512]{1,0:T(8,128)(2,1)S(1)}, u32[]{:S(2)}, u32[]{:S(2)}) collective-permute-start(bf16[32,512]{1,0:T(8,128)(2,1)S(1)} %select_bitcast_fusion.3), channel_id=1, source_target_pairs={{4,0},{8,4},{12,8},{16,12},{20,16},{24,20},{28,24},{0,28},{5,1},{9... | collective-permute-start | bytes 98312 | tf_op jit(solution)/shard_map/ppermute | solution.py:12
  20.8 31.8 %copy-start = (f32[1,32,512]{2,1,0:T(8,128)S(1)}, f32[1,32,512]{2,1,0:T(8,128)}, u32[]{:S(2)}) copy-start(f32[1,32,512]{2,1,0:T(8,128)} %param.13) | copy-start | bytes 196612
  26.8 7.1 %collective-permute-start.1 = (f32[32,512]{1,0:T(8,128)S(1)}, f32[32,512]{1,0:T(8,128)S(1)}, u32[]{:S(2)}, u32[]{:S(2)}) collective-permute-start(f32[32,512]{1,0:T(8,128)S(1)} %slice.61), channel_id=1, source_target_pairs={{28,0},{0,4},{4,8},{8,12},{12,16},{16,20},{20,24},{24,28},{29,1},{... | collective-permute-start | bytes 196616 | tf_op jit(solution)/shard_map/ppermute | solution.py:12
  36.8 4.0 %collective-permute-start.2 = (bf16[32,512]{1,0:T(8,128)(2,1)S(1)}, bf16[32,512]{1,0:T(8,128)(2,1)S(1)}, u32[]{:S(2)}, u32[]{:S(2)}) collective-permute-start(bf16[32,512]{1,0:T(8,128)(2,1)S(1)} %select_bitcast_fusion.2), channel_id=1, source_target_pairs={{4,0},{8,4},{12,8},{16,12},{20,16},{24,20},{28,24},{0,28},{5,1},{9... | collective-permute-start | bytes 98312 | tf_op jit(solution)/shard_map/ppermute | solution.py:12
  52.5 7.1 %collective-permute-start.3 = (f32[32,512]{1,0:T(8,128)S(1)}, f32[32,512]{1,0:T(8,128)S(1)}, u32[]{:S(2)}, u32[]{:S(2)}) collective-permute-start(f32[32,512]{1,0:T(8,128)S(1)} %slice.63), channel_id=1, source_target_pairs={{28,0},{0,4},{4,8},{8,12},{12,16},{16,20},{20,24},{24,28},{29,1},{... | collective-permute-start | bytes 196616 | tf_op jit(solution)/shard_map/ppermute | solution.py:12
  110.4 5.7 %collective-permute-start.4 = (bf16[32,512]{1,0:T(8,128)(2,1)S(1)}, bf16[32,512]{1,0:T(8,128)(2,1)S(1)}, u32[]{:S(2)}, u32[]{:S(2)}) collective-permute-start(bf16[32,512]{1,0:T(8,128)(2,1)S(1)} %select_bitcast_fusion.1), channel_id=1, source_target_pairs={{4,0},{8,4},{12,8},{16,12},{20,16},{24,20},{28,24},{0,28},{5,1},{9... | collective-permute-start | bytes 98312 | tf_op jit(solution)/shard_map/ppermute | solution.py:12
  127.8 7.8 %collective-permute-start.5 = (f32[32,512]{1,0:T(8,128)S(1)}, f32[32,512]{1,0:T(8,128)S(1)}, u32[]{:S(2)}, u32[]{:S(2)}) collective-permute-start(f32[32,512]{1,0:T(8,128)S(1)} %slice.65), channel_id=1, source_target_pairs={{28,0},{0,4},{4,8},{8,12},{12,16},{16,20},{20,24},{24,28},{29,1},{... | collective-permute-start | bytes 196616 | tf_op jit(solution)/shard_map/ppermute | solution.py:12
  177.7 5.0 %collective-permute-start.6 = (bf16[32,512]{1,0:T(8,128)(2,1)S(1)}, bf16[32,512]{1,0:T(8,128)(2,1)S(1)}, u32[]{:S(2)}, u32[]{:S(2)}) collective-permute-start(bf16[32,512]{1,0:T(8,128)(2,1)S(1)} %select_bitcast_fusion), channel_id=1, source_target_pairs={{4,0},{8,4},{12,8},{16,12},{20,16},{24,20},{28,24},{0,28},{5,1},{9... | collective-permute-start | bytes 98312 | tf_op jit(solution)/shard_map/ppermute | solution.py:12
  194.4 7.7 %collective-permute-start.7 = (f32[32,512]{1,0:T(8,128)S(1)}, f32[32,512]{1,0:T(8,128)S(1)}, u32[]{:S(2)}, u32[]{:S(2)}) collective-permute-start(f32[32,512]{1,0:T(8,128)S(1)} %slice.67), channel_id=1, source_target_pairs={{28,0},{0,4},{4,8},{8,12},{12,16},{16,20},{20,24},{24,28},{29,1},{... | collective-permute-start | bytes 196616 | tf_op jit(solution)/shard_map/ppermute | solution.py:12
where the time goes:
time: 251 us; the launch traced here: 250 us
  blocking collectives  136 us (54%)
  waiting for transfers between devices  28.5 us (11%)
  matrix products  28.4 us (11%)
  other arithmetic  26.8 us (11%)
  starting transfers between devices  17.7 us (7%)
  local copies, waits for them, and re-layouts  11.8 us (5%)
    psum x3, blocking collectives, gram(): total = lax.psum(partial_sum, ('sx', 'sy'))  113 us
    ppermute x8, waiting for transfers between devices, passed_along(): return lax.ppermute(block, axis, route)  28.5 us
    dot_general x4, matrix products, apply_op(): lax.dot_general(lax.all_gather(local, 'sy', axis=1, tiled=True), matrix,...  23.8 us
    all_gather x4, blocking collectives, apply_op(): lax.all_gather(local, 'sy', axis=1, tiled=True)  23.1 us
    ppermute x8, starting transfers between devices, passed_along(): return lax.ppermute(block, axis, route)  17.7 us
    another operation x9, other arithmetic, solve_spd(): lower = jnp.linalg.cholesky(matrix)  10.8 us
    another operation x6, other arithmetic, solve_spd(): return jax.scipy.linalg.cho_solve((lower, True), rhs)  9.26 us
    gather x8, local copies, waits for them, and re-layouts, apply_op(): sent = jnp.take(block, match_loc, axis=1)  5.68 us
  transfers between devices with their start and end apart: 8, of which 7 were waited for; matrix products, arithmetic and copies ran while one was open for 3% of the time, Pallas kernels for 0%

commit v1 on v0

--- a/solution.py
+++ b/solution.py
@@ -19,7 +19,9 @@
     right_part = passed_along(sent, "sx", -1)
     local = jnp.concatenate([block, right_part], axis=1)
     prod = lax.dot_general(
-        lax.all_gather(local, "sy", axis=1, tiled=True),
+        jnp.concatenate(
+            lax.all_to_all(jnp.stack([local] * lax.axis_size("sy")), "sy", 0, 0), axis=1
+        ),
         matrix,
         (((1,), (1,)), ((), ())),
         preferred_element_type=jnp.float32,

time: 251 us -> 262 us (1.044)
  waiting for transfers between devices: 28.5 us -> 39.7 us
  blocking collectives: 136 us -> 129 us
  starting transfers between devices: 17.7 us -> 23.1 us
    all_gather x4 -> x0, blocking collectives: 23.1 us -> none  [apply_op(): lax.all_gather(local, 'sy', axis=1, tiled=True)]
    all_to_all x0 -> x2, blocking collectives: none -> 16.8 us  [apply_op(): lax.all_to_all(jnp.stack([local] * lax.axis_size('sy')), 'sy', 0, 0)]
    all_to_all x0 -> x2, waiting for transfers between devices: none -> 11.3 us  [apply_op(): lax.all_to_all(jnp.stack([local] * lax.axis_size('sy')), 'sy', 0, 0)]
    all_to_all x0 -> x2, starting transfers between devices: none -> 6.81 us  [apply_op(): lax.all_to_all(jnp.stack([local] * lax.axis_size('sy')), 'sy', 0, 0)]
  transfers between devices with their start and end apart: 8 -> 10, of which waited for: 7 -> 8; matrix products, arithmetic and copies ran while one was open for 3% -> 4% of each run, Pallas kernels for 0% -> 0%
where the time goes in v1:
time: 262 us; the launch traced here: 261 us
  blocking collectives  129 us (49%)
  waiting for transfers between devices  39.7 us (15%)
  matrix products  28.3 us (11%)
  other arithmetic  26.8 us (10%)
  starting transfers between devices  23.1 us (9%)
  local copies, waits for them, and re-layouts  13.3 us (5%)
    psum x3, blocking collectives, gram(): total = lax.psum(partial_sum, ('sx', 'sy'))  112 us
    ppermute x8, waiting for transfers between devices, passed_along(): return lax.ppermute(block, axis, route)  28.4 us
    dot_general x4, matrix products, apply_op(): lax.dot_general(jnp.concatenate(lax.all_to_all(jnp.stack([local] * lax.ax...  23.8 us
    all_to_all x2, blocking collectives, apply_op(): lax.all_to_all(jnp.stack([local] * lax.axis_size('sy')), 'sy', 0, 0)  16.8 us
    ppermute x8, starting transfers between devices, passed_along(): return lax.ppermute(block, axis, route)  16.3 us
    all_to_all x2, waiting for transfers between devices, apply_op(): lax.all_to_all(jnp.stack([local] * lax.axis_size('sy')), 'sy', 0, 0)  11.3 us
    another operation x9, other arithmetic, solve_spd(): lower = jnp.linalg.cholesky(matrix)  10.8 us
    another operation x6, other arithmetic, solve_spd(): return jax.scipy.linalg.cho_solve((lower, True), rhs)  9.26 us
  transfers between devices with their start and end apart: 10, of which 8 were waited for; matrix products, arithmetic and copies ran while one was open for 4% of the time, Pallas kernels for 0%

profile of v1, /device:TPU:0, one launch (start us, length us, event | category | flops | bytes accessed | tf_op | source)
XLA Modules:
  0.0 261.0 jit_solution(14725554903969084018)
XLA Ops:
  4.4 6.1 %collective-permute-start = (bf16[32,512]{1,0:T(8,128)(2,1)S(1)}, bf16[32,512]{1,0:T(8,128)(2,1)S(1)}, u32[]{:S(2)}, u32[]{:S(2)}) collective-permute-start(bf16[32,512]{1,0:T(8,128)(2,1)S(1)} %select_bitcast_fusion.3), channel_id=1, source_target_pairs={{4,0},{8,4},{12,8},{16,12},{20,16},{24,20},{28,24},{0,28},{5,1},{9... | collective-permute-start | bytes 98312 | tf_op jit(solution)/shard_map/ppermute | solution.py:12
  10.5 4.4 %sort.17 = (s32[512]{0:T(512)}, s32[512]{0:T(512)S(1)}) sort(s32[512]{0:T(512)} %bitcast.141, s32[512]{0:T(512)S(1)} %iota.35), dimensions={0}, to_apply=%region_0.2 | sort | flops 4608 | bytes 8192 | tf_op jit(solution)/shard_map/jit(argsort)/sort | solution.py:54
  15.7 3.4 %all-to-all-start = ((bf16[4,32,1024]{2,1,0:T(8,128)(2,1)}), bf16[4,32,1024]{2,1,0:T(8,128)(2,1)S(1)}, u32[]{:S(2)}, u32[]{:S(2)}) async-start(bf16[4,32,1024]{2,1,0:T(8,128)(2,1)} %stack.8), calls=%async_computation | async-start | bytes 524288 | tf_op jit(solution)/shard_map/all_to_all | solution.py:23
  19.1 6.0 %all-to-all-done = bf16[4,32,1024]{2,1,0:T(8,128)(2,1)S(1)} async-done(((bf16[4,32,1024]{2,1,0:T(8,128)(2,1)}), bf16[4,32,1024]{2,1,0:T(8,128)(2,1)S(1)}, u32[]{:S(2)}, u32[]{:S(2)}) %all-to-all-start) | async-done | bytes 262176 | tf_op jit(solution)/shard_map/all_to_all | solution.py:23
  25.1 6.0 %fusion.6 = f32[32,1024]{1,0:T(8,128)S(1)} fusion(bf16[32,4096]{1,0:T(8,128)(2,1)S(1)} %bitcast.131, bf16[1,1024,4096]{2,1,0:T(8,128)(2,1)} %param.12), kind=kOutput, calls=%fused_computation.14 | convolution fusion | flops 268435456 | bytes 8781824 | tf_op jit(solution)/shard_map/dot_general | solution.py:21
  31.2 6.9 %collective-permute-done.1 = f32[32,512]{1,0:T(8,128)S(1)} collective-permute-done((f32[32,512]{1,0:T(8,128)S(1)}, f32[32,512]{1,0:T(8,128)S(1)}, u32[]{:S(2)}, u32[]{:S(2)}) %collective-permute-start.1) | collective-permute-done | bytes 65568 | tf_op jit(solution)/shard_map/ppermute | solution.py:12
  41.1 3.9 %collective-permute-done.2 = bf16[32,512]{1,0:T(8,128)(2,1)S(1)} collective-permute-done((bf16[32,512]{1,0:T(8,128)(2,1)S(1)}, bf16[32,512]{1,0:T(8,128)(2,1)S(1)}, u32[]{:S(2)}, u32[]{:S(2)}) %collective-permute-start.2) | collective-permute-done | bytes 32800 | tf_op jit(solution)/shard_map/ppermute | solution.py:12
  45.0 8.4 %all_to_all.20 = bf16[4,32,1024]{2,1,0:T(8,128)(2,1)S(1)} all-to-all(bf16[4,32,1024]{2,1,0:T(8,128)(2,1)S(1)} %stack.9), channel_id=1, replica_groups=mesh['sx'=8,'sy'=4] {'sy'}, dimensions={0} | all-to-all | bytes 524288 | tf_op jit(solution)/shard_map/all_to_all | solution.py:23
  53.4 6.0 %fusion.2 = f32[32,1024]{1,0:T(8,128)S(1)} fusion(bf16[32,4096]{1,0:T(8,128)(2,1)S(1)} %bitcast.132, bf16[1,1024,4096]{2,1,0:T(8,128)(2,1)} %param.11), kind=kOutput, calls=%fused_computation.10 | convolution fusion | flops 268435456 | bytes 8781824 | tf_op jit(solution)/shard_map/dot_general | solution.py:21
  59.7 6.7 %collective-permute-done.3 = f32[32,512]{1,0:T(8,128)S(1)} collective-permute-done((f32[32,512]{1,0:T(8,128)S(1)}, f32[32,512]{1,0:T(8,128)S(1)}, u32[]{:S(2)}, u32[]{:S(2)}) %collective-permute-start.3) | collective-permute-done | bytes 65568 | tf_op jit(solution)/shard_map/ppermute | solution.py:12
  67.9 37.1 %all-reduce = (f32[32,32]{1,0:T(8,128)S(1)}, f32[32,32]{1,0:T(8,128)S(1)}) all-reduce(f32[32,32]{1,0:T(8,128)S(1)} %convolution_bitcast_fusion, f32[32,32]{1,0:T(8,128)S(1)} %fusion.11), channel_id=1, replica_groups=mesh['sx'=8,'sy'=4] {'sx','sy'}, use_global_device_ids=true, to_apply=%region_4.8 | all-reduce | flops 2048 | bytes 16384 | tf_op jit(solution)/shard_map/psum | solution.py:37
  105.2 2.9 %cholesky.59 = f32[32,32]{1,0:T(8,128)S(1)} custom-call(f32[32,32]{1,0:T(8,128)S(1)} %fusion.34), custom_call_target="Cholesky" | custom-call | tf_op jit(solution)/shard_map/jit(cholesky)/cholesky | solution.py:42
  114.2 4.1 %collective-permute-start.4 = (bf16[32,512]{1,0:T(8,128)(2,1)S(1)}, bf16[32,512]{1,0:T(8,128)(2,1)S(1)}, u32[]{:S(2)}, u32[]{:S(2)}) collective-permute-start(bf16[32,512]{1,0:T(8,128)(2,1)S(1)} %select_bitcast_fusion.1), channel_id=1, source_target_pairs={{4,0},{8,4},{12,8},{16,12},{20,16},{24,20},{28,24},{0,28},{5,1},{9... | collective-permute-start | bytes 98312 | tf_op jit(solution)/shard_map/ppermute | solution.py:12
  122.0 3.4 %all-to-all-start.2 = ((bf16[4,32,1024]{2,1,0:T(8,128)(2,1)}), bf16[4,32,1024]{2,1,0:T(8,128)(2,1)S(1)}, u32[]{:S(2)}, u32[]{:S(2)}) async-start(bf16[4,32,1024]{2,1,0:T(8,128)(2,1)} %stack.10), calls=%async_computation.2 | async-start | bytes 524288 | tf_op jit(solution)/shard_map/all_to_all | solution.py:23
  126.0 5.3 %all-to-all-done.2 = bf16[4,32,1024]{2,1,0:T(8,128)(2,1)S(1)} async-done(((bf16[4,32,1024]{2,1,0:T(8,128)(2,1)}), bf16[4,32,1024]{2,1,0:T(8,128)(2,1)S(1)}, u32[]{:S(2)}, u32[]{:S(2)}) %all-to-all-start.2) | async-done | bytes 262176 | tf_op jit(solution)/shard_map/all_to_all | solution.py:23
  131.4 6.0 %fusion.4 = f32[32,1024]{1,0:T(8,128)S(1)} fusion(bf16[32,4096]{1,0:T(8,128)(2,1)S(1)} %bitcast.133, bf16[1,1024,4096]{2,1,0:T(8,128)(2,1)} %param.12), kind=kOutput, calls=%fused_computation.12 | convolution fusion | flops 268435456 | bytes 8781824 | tf_op jit(solution)/shard_map/dot_general | solution.py:21
  140.8 3.7 %collective-permute-done.5 = f32[32,512]{1,0:T(8,128)S(1)} collective-permute-done((f32[32,512]{1,0:T(8,128)S(1)}, f32[32,512]{1,0:T(8,128)S(1)}, u32[]{:S(2)}, u32[]{:S(2)}) %collective-permute-start.5) | collective-permute-done | bytes 65568 | tf_op jit(solution)/shard_map/ppermute | solution.py:12
  146.0 37.2 %psum.30 = f32[32,32]{1,0:T(8,128)S(1)} all-reduce(f32[32,32]{1,0:T(8,128)S(1)} %fusion.12), channel_id=1, replica_groups=mesh['sx'=8,'sy'=4] {'sx','sy'}, use_global_device_ids=true, to_apply=%region_5.10 | all-reduce | flops 1024 | bytes 8192 | tf_op jit(solution)/shard_map/psum | solution.py:37
  185.5 4.1 %collective-permute-start.6 = (bf16[32,512]{1,0:T(8,128)(2,1)S(1)}, bf16[32,512]{1,0:T(8,128)(2,1)S(1)}, u32[]{:S(2)}, u32[]{:S(2)}) collective-permute-start(bf16[32,512]{1,0:T(8,128)(2,1)S(1)} %select_bitcast_fusion), channel_id=1, source_target_pairs={{4,0},{8,4},{12,8},{16,12},{20,16},{24,20},{28,24},{0,28},{5,1},{9... | collective-permute-start | bytes 98312 | tf_op jit(solution)/shard_map/ppermute | solution.py:12
  191.2 8.4 %all_to_all.21 = bf16[4,32,1024]{2,1,0:T(8,128)(2,1)S(1)} all-to-all(bf16[4,32,1024]{2,1,0:T(8,128)(2,1)S(1)} %stack.11), channel_id=1, replica_groups=mesh['sx'=8,'sy'=4] {'sy'}, dimensions={0} | all-to-all | bytes 524288 | tf_op jit(solution)/shard_map/all_to_all | solution.py:23
  199.6 6.0 %fusion = f32[32,1024]{1,0:T(8,128)S(1)} fusion(bf16[32,4096]{1,0:T(8,128)(2,1)S(1)} %bitcast.134, bf16[1,1024,4096]{2,1,0:T(8,128)(2,1)} %param.11), kind=kOutput, calls=%fused_computation.8 | convolution fusion | flops 268435456 | bytes 8781824 | tf_op jit(solution)/shard_map/dot_general | solution.py:21
  207.4 5.5 %collective-permute-done.7 = f32[32,512]{1,0:T(8,128)S(1)} collective-permute-done((f32[32,512]{1,0:T(8,128)S(1)}, f32[32,512]{1,0:T(8,128)S(1)}, u32[]{:S(2)}, u32[]{:S(2)}) %collective-permute-start.7) | collective-permute-done | bytes 65568 | tf_op jit(solution)/shard_map/ppermute | solution.py:12
  214.4 37.6 %psum.31 = f32[32,32]{1,0:T(8,128)S(1)} all-reduce(f32[32,32]{1,0:T(8,128)S(1)} %fusion.13), channel_id=1, replica_groups=mesh['sx'=8,'sy'=4] {'sx','sy'}, use_global_device_ids=true, to_apply=%region_6.11 | all-reduce | flops 1024 | bytes 8192 | tf_op jit(solution)/shard_map/psum | solution.py:37
  252.2 2.9 %cholesky.81 = f32[32,32]{1,0:T(8,128)S(1)} custom-call(f32[32,32]{1,0:T(8,128)S(1)} %fusion.21), custom_call_target="Cholesky" | custom-call | tf_op jit(solution)/shard_map/jit(cholesky)/cholesky | solution.py:42
  (103 shorter events, 38.1 us)
Async XLA Ops:
  4.4 10.5 %collective-permute-start = (bf16[32,512]{1,0:T(8,128)(2,1)S(1)}, bf16[32,512]{1,0:T(8,128)(2,1)S(1)}, u32[]{:S(2)}, u32[]{:S(2)}) collective-permute-start(bf16[32,512]{1,0:T(8,128)(2,1)S(1)} %select_bitcast_fusion.3), channel_id=1, source_target_pairs={{4,0},{8,4},{12,8},{16,12},{20,16},{24,20},{28,24},{0,28},{5,1},{9... | collective-permute-start | bytes 98312 | tf_op jit(solution)/shard_map/ppermute | solution.py:12
  15.7 9.4 %all-to-all-start = ((bf16[4,32,1024]{2,1,0:T(8,128)(2,1)}), bf16[4,32,1024]{2,1,0:T(8,128)(2,1)S(1)}, u32[]{:S(2)}, u32[]{:S(2)}) async-start(bf16[4,32,1024]{2,1,0:T(8,128)(2,1)} %stack.8), calls=%async_computation | async-start | bytes 524288 | tf_op jit(solution)/shard_map/all_to_all | solution.py:23
  31.1 28.4 %copy-start = (f32[1,32,512]{2,1,0:T(8,128)S(1)}, f32[1,32,512]{2,1,0:T(8,128)}, u32[]{:S(2)}) copy-start(f32[1,32,512]{2,1,0:T(8,128)} %param.13) | copy-start | bytes 196612
  31.1 7.0 %collective-permute-start.1 = (f32[32,512]{1,0:T(8,128)S(1)}, f32[32,512]{1,0:T(8,128)S(1)}, u32[]{:S(2)}, u32[]{:S(2)}) collective-permute-start(f32[32,512]{1,0:T(8,128)S(1)} %slice.61), channel_id=1, source_target_pairs={{28,0},{0,4},{4,8},{8,12},{12,16},{16,20},{20,24},{24,28},{29,1},{... | collective-permute-start | bytes 196616 | tf_op jit(solution)/shard_map/ppermute | solution.py:12
  41.0 4.0 %collective-permute-start.2 = (bf16[32,512]{1,0:T(8,128)(2,1)S(1)}, bf16[32,512]{1,0:T(8,128)(2,1)S(1)}, u32[]{:S(2)}, u32[]{:S(2)}) collective-permute-start(bf16[32,512]{1,0:T(8,128)(2,1)S(1)} %select_bitcast_fusion.2), channel_id=1, source_target_pairs={{4,0},{8,4},{12,8},{16,12},{20,16},{24,20},{28,24},{0,28},{5,1},{9... | collective-permute-start | bytes 98312 | tf_op jit(solution)/shard_map/ppermute | solution.py:12
  59.4 7.0 %collective-permute-start.3 = (f32[32,512]{1,0:T(8,128)S(1)}, f32[32,512]{1,0:T(8,128)S(1)}, u32[]{:S(2)}, u32[]{:S(2)}) collective-permute-start(f32[32,512]{1,0:T(8,128)S(1)} %slice.63), channel_id=1, source_target_pairs={{28,0},{0,4},{4,8},{8,12},{12,16},{16,20},{20,24},{24,28},{29,1},{... | collective-permute-start | bytes 196616 | tf_op jit(solution)/shard_map/ppermute | solution.py:12
  114.2 7.0 %collective-permute-start.4 = (bf16[32,512]{1,0:T(8,128)(2,1)S(1)}, bf16[32,512]{1,0:T(8,128)(2,1)S(1)}, u32[]{:S(2)}, u32[]{:S(2)}) collective-permute-start(bf16[32,512]{1,0:T(8,128)(2,1)S(1)} %select_bitcast_fusion.1), channel_id=1, source_target_pairs={{4,0},{8,4},{12,8},{16,12},{20,16},{24,20},{28,24},{0,28},{5,1},{9... | collective-permute-start | bytes 98312 | tf_op jit(solution)/shard_map/ppermute | solution.py:12
  122.0 9.4 %all-to-all-start.2 = ((bf16[4,32,1024]{2,1,0:T(8,128)(2,1)}), bf16[4,32,1024]{2,1,0:T(8,128)(2,1)S(1)}, u32[]{:S(2)}, u32[]{:S(2)}) async-start(bf16[4,32,1024]{2,1,0:T(8,128)(2,1)} %stack.10), calls=%async_computation.2 | async-start | bytes 524288 | tf_op jit(solution)/shard_map/all_to_all | solution.py:23
  137.4 7.2 %collective-permute-start.5 = (f32[32,512]{1,0:T(8,128)S(1)}, f32[32,512]{1,0:T(8,128)S(1)}, u32[]{:S(2)}, u32[]{:S(2)}) collective-permute-start(f32[32,512]{1,0:T(8,128)S(1)} %slice.65), channel_id=1, source_target_pairs={{28,0},{0,4},{4,8},{8,12},{12,16},{16,20},{20,24},{24,28},{29,1},{... | collective-permute-start | bytes 196616 | tf_op jit(solution)/shard_map/ppermute | solution.py:12
  185.5 5.7 %collective-permute-start.6 = (bf16[32,512]{1,0:T(8,128)(2,1)S(1)}, bf16[32,512]{1,0:T(8,128)(2,1)S(1)}, u32[]{:S(2)}, u32[]{:S(2)}) collective-permute-start(bf16[32,512]{1,0:T(8,128)(2,1)S(1)} %select_bitcast_fusion), channel_id=1, source_target_pairs={{4,0},{8,4},{12,8},{16,12},{20,16},{24,20},{28,24},{0,28},{5,1},{9... | collective-permute-start | bytes 98312 | tf_op jit(solution)/shard_map/ppermute | solution.py:12
  205.6 7.3 %collective-permute-start.7 = (f32[32,512]{1,0:T(8,128)S(1)}, f32[32,512]{1,0:T(8,128)S(1)}, u32[]{:S(2)}, u32[]{:S(2)}) collective-permute-start(f32[32,512]{1,0:T(8,128)S(1)} %slice.67), channel_id=1, source_target_pairs={{28,0},{0,4},{4,8},{8,12},{12,16},{16,20},{20,24},{24,28},{29,1},{... | collective-permute-start | bytes 196616 | tf_op jit(solution)/shard_map/ppermute | solution.py:12
